TPU v7x, 32 devices: a whole 2x2x4 slice. The times are simulated.
32 devices in a mesh: dp: 4 (over z), expert: 8 (over y, x, core).
Axes of the slice: x: 2, y: 2, z: 4, core: 2. Of those that a mesh axis runs over, the one named last changes fastest.
Arguments:
- tokens: bfloat16 [8, 512, 1024], P('expert', 'dp'), may hold values from -6 to 6
- qkv_weight: bfloat16 [1024, 3072], P(('dp', 'expert')), may hold values from -0.1875 to 0.1875
- proj_weight: bfloat16 [1024, 1024], P(('dp', 'expert')), may hold values from -0.75 to 0.75
- router_weight: bfloat16 [1024, 8], P(('dp', 'expert')), may hold values from -0.09375 to 0.09375
- norm_gains: bfloat16 [2, 1024], P(None, ('dp', 'expert')), may hold values from 0.5 to 1.5
- biases: bfloat16 [5, 1024], P(None, ('dp', 'expert')), may hold values from -1.1953125 to 1.1953125
- up_weight: bfloat16 [8, 1024, 4096], P('expert', None, 'dp'), may hold values from -0.1875 to 0.1875
- up_bias: bfloat16 [8, 4096], P('expert', 'dp'), may hold values from -1.1953125 to 1.1953125
- down_weight: bfloat16 [8, 4096, 1024], P('expert', 'dp'), may hold values from -0.75 to 0.75
- down_bias: bfloat16 [8, 1024], P('expert', 'dp'), may hold values from -6 to 6
- routes: int32 [8, 512, 1], P('expert', 'dp'), may hold values from 0 to 7
- slot_order: int32 [8, 4, 128], P('expert', 'dp'), may hold values from 0 to 127, each once within a row
- segments: int32 [8, 512], P('expert'), may hold values from 0 to 6, never falling along the last dimension, each value on 1 to 256 neighbouring positions
- parents: int32 [8, 7], P('expert'), may hold values from 0 to 5, as said below
- cotangent: bfloat16 [8, 512, 1024], P('expert', 'dp'), may hold values from -6 to 6
Outputs:
- outputs: bfloat16 [8, 512, 1024], P('expert', 'dp')
- grad_tokens: float32 [8, 512, 1024], P('expert', 'dp')
- grad_qkv: float32 [1024, 3072], P(('dp', 'expert'))
- grad_proj: float32 [1024, 1024], P(('dp', 'expert'))
- grad_router: float32 [1024, 8], P(('dp', 'expert'))
- grad_gains: float32 [2, 1024], P(None, ('dp', 'expert'))
- grad_biases: float32 [5, 1024], P(None, ('dp', 'expert'))
- grad_up: float32 [8, 1024, 4096], P('expert', None, 'dp')
- grad_up_bias: float32 [8, 4096], P('expert', 'dp')
- grad_down: float32 [8, 4096, 1024], P('expert', 'dp')
- grad_down_bias: float32 [8, 1024], P('expert', 'dp')
Inputs may be any that keep to these rules, and one draw needn't show every extreme that they name: Along each tree the segment number never falls, every one of the 7 segments has a token, and the longest has 256. parents[t, 0] = 0, parents[t, s] < s for every other s, and the last segment's parent is segment 7 - 2. `routes`: every expert is the route of some token. `slot_order`: each device's 128 tokens hold every priority once.
All inputs are finite; a program needn't handle non-finite values.
Results may differ from a plain program's by a relative error of at most 0.014.
Values may be sent and summed in bfloat16 or wider, within the bound.
No kernel may reach another device: no remote copies, remote signals or barrier semaphores. Data moves between devices by JAX's collectives and lax.ppermute only.
A program may use at most 192 MiB of HBM per device.

v0:
```python
from functools import partial
import math
import jax
import jax.numpy as jnp
from jax import lax
from jax.sharding import PartitionSpec as P

H = 16
NSEG = 7
EPS = 1e-05
NEG = -1e30
HIGH = lax.Precision.HIGHEST


def layer_norm(values, gain, shift):
    mean = jnp.mean(values, axis=-1, keepdims=True)
    centred = values - mean
    spread = jnp.mean(centred * centred, axis=-1, keepdims=True)
    return centred * lax.rsqrt(spread + EPS) * gain + shift


def ancestry(parents, number):
    labels = jnp.arange(number, dtype=jnp.int32)
    direct = (labels[None, :] == parents[:, None]).astype(jnp.float32)
    reach = jnp.minimum(direct + jnp.eye(number, dtype=jnp.float32), 1.0)
    for step in range(3):
        reach = jnp.minimum(jnp.dot(reach, reach, precision=HIGH), 1.0)
    return reach


def slot_table(route_ids, order, experts, capacity):
    labels = jnp.arange(experts, dtype=jnp.int32)
    expert_hot = route_ids[:, None] == labels[None, :]
    same = route_ids[:, None] == route_ids[None, :]
    before = order[None, :] < order[:, None]
    rank = jnp.sum((same & before).astype(jnp.int32), axis=1)
    slot_hot = rank[:, None] == jnp.arange(capacity, dtype=jnp.int32)[None, :]
    table = expert_hot[:, :, None] & slot_hot[:, None, :]
    return (expert_hot.astype(jnp.float32), table)


def expert_gate(logits, expert_hot):
    return jnp.sum(jax.nn.softmax(logits, axis=-1) * expert_hot, axis=-1)


def tanh_gelu(values):
    return jax.nn.gelu(values, approximate=True)


def shards(
    tokens,
    qkv_weight,
    proj_weight,
    router_weight,
    norm_gains,
    biases,
    up_weight,
    up_bias,
    down_weight,
    down_bias,
    routes,
    slot_order,
    segments,
    parents,
    cotangent,
):
    qkv_full, proj_full, router_full, gain_full, bias_full = (
        lax.all_gather(qkv_weight, ("dp", "expert"), axis=0, tiled=True),
        lax.all_gather(proj_weight, ("dp", "expert"), axis=0, tiled=True),
        lax.all_gather(router_weight, ("dp", "expert"), axis=0, tiled=True),
        lax.all_gather(norm_gains, ("dp", "expert"), axis=1, tiled=True),
        lax.all_gather(biases, ("dp", "expert"), axis=1, tiled=True),
    )
    up_full, up_shift, down_full, down_shift = (
        lax.all_gather(up_weight, "dp", axis=2, tiled=True),
        lax.all_gather(up_bias, "dp", axis=1, tiled=True),
        lax.all_gather(down_weight, "dp", axis=1, tiled=True),
        lax.all_gather(down_bias, "dp", axis=1, tiled=True),
    )
    rows = tokens.shape[1]
    width = tokens.shape[2]
    head_dim = width // H
    scale = head_dim ** (-0.5)
    experts = router_full.shape[1]
    capacity = (9 * rows + 8 * experts - 1) // (8 * experts)
    gain32 = gain_full.astype(jnp.float32)
    bias32 = bias_full.astype(jnp.float32)
    inputs = tokens[0].astype(jnp.float32)
    normed, norm1_back = jax.vjp(layer_norm, inputs, gain32[0], bias32[0])
    normed_low = normed.astype(jnp.bfloat16)
    shift = jnp.concatenate([bias32[1], jnp.zeros((width,), jnp.float32), bias32[2]])
    packed = (jnp.dot(normed_low, qkv_full, preferred_element_type=jnp.float32) + shift).astype(
        jnp.bfloat16
    )
    key_value = lax.all_gather(packed[:, width:], "dp", axis=0, tiled=True)
    length = key_value.shape[0]
    start = lax.axis_index("dp") * rows
    query_pos = start + jnp.arange(rows, dtype=jnp.int32)
    reach = ancestry(parents[0], NSEG)
    labels = jnp.arange(NSEG, dtype=jnp.int32)
    key_hot = (segments[0][:, None] == labels[None, :]).astype(jnp.float32)
    query_reach = jnp.dot(lax.dynamic_slice_in_dim(key_hot, start, rows, 0), reach, precision=HIGH)
    block = math.gcd(length, 512)
    number = length // block
    hot_blocks = key_hot.reshape(number, block, NSEG)
    pos_blocks = jnp.arange(length, dtype=jnp.int32).reshape(number, block)
    query_heads = packed[:, :width].reshape(rows, H, head_dim)

    def block_scores(key_blk, hot_blk, pos_blk):
        allowed = (jnp.dot(query_reach, hot_blk.T, precision=HIGH) > 0.5) & (
            pos_blk[None, :] <= query_pos[:, None]
        )
        raw = (
            jnp.einsum("qhd,khd->hqk", query_heads, key_blk, preferred_element_type=jnp.float32)
            * scale
        )
        return jnp.where(allowed[None], raw, NEG)

    def split_blocks(pairs):
        keys = pairs[:, :width].reshape(number, block, H, head_dim)
        values = pairs[:, width:].reshape(number, block, H, head_dim)
        return (keys, values)

    key_blocks, value_blocks = split_blocks(key_value)

    def total_step(carry, item):
        top, total = carry
        scores = block_scores(item[0], item[1], item[2])
        new_top = jnp.maximum(top, jnp.max(scores, axis=-1))
        total = total * jnp.exp(top - new_top) + jnp.sum(
            jnp.exp(scores - new_top[:, :, None]), axis=-1
        )
        return ((new_top, total), None)

    first_carry = (jnp.full((H, rows), NEG, jnp.float32), jnp.zeros((H, rows), jnp.float32))
    (top, total), unused = lax.scan(total_step, first_carry, (key_blocks, hot_blocks, pos_blocks))
    log_total = top + jnp.log(total)

    def value_step(accum, item):
        scores = block_scores(item[0], item[1], item[2])
        probs = jnp.exp(scores - log_total[:, :, None]).astype(jnp.bfloat16)
        return (
            accum + jnp.einsum("hqk,khd->qhd", probs, item[3], preferred_element_type=jnp.float32),
            None,
        )

    attended32, unused = lax.scan(
        value_step,
        jnp.zeros((rows, H, head_dim), jnp.float32),
        (key_blocks, hot_blocks, pos_blocks, value_blocks),
    )
    attended_low = attended32.reshape(rows, width).astype(jnp.bfloat16)
    mixed = (
        inputs + jnp.dot(attended_low, proj_full, preferred_element_type=jnp.float32) + bias32[3]
    )
    normed2, norm2_back = jax.vjp(layer_norm, mixed, gain32[1], bias32[4])
    normed2_low = normed2.astype(jnp.bfloat16)
    logits = jnp.dot(normed2_low, router_full, preferred_element_type=jnp.float32)
    expert_hot, table = slot_table(routes[0, :, 0], slot_order[0, 0], experts, capacity)
    gate, gate_back = jax.vjp(partial(expert_gate, expert_hot=expert_hot), logits)
    table_low = table.astype(jnp.bfloat16)
    sent = jnp.einsum(
        "tec,td->ecd", table_low, normed2_low, preferred_element_type=jnp.float32
    ).astype(jnp.bfloat16)
    arrived = lax.all_to_all(sent, "expert", split_axis=0, concat_axis=0, tiled=True)
    slots = arrived.reshape(-1, width)
    pre = jnp.dot(slots, up_full[0], preferred_element_type=jnp.float32) + up_shift[0].astype(
        jnp.float32
    )
    act, act_back = jax.vjp(tanh_gelu, pre)
    act_low = act.astype(jnp.bfloat16)
    result = (
        jnp.dot(act_low, down_full[0], preferred_element_type=jnp.float32)
        + down_shift[0].astype(jnp.float32)
    ).astype(jnp.bfloat16)
    returned = lax.all_to_all(
        result.reshape(arrived.shape), "expert", split_axis=0, concat_axis=0, tiled=True
    )
    combined = jnp.einsum("tec,ecd->td", table_low, returned, preferred_element_type=jnp.float32)
    outputs = (mixed + gate[:, None] * combined).astype(jnp.bfloat16)
    qkv_full, proj_full, router_full = (
        lax.all_gather(qkv_weight, ("dp", "expert"), axis=0, tiled=True),
        lax.all_gather(proj_weight, ("dp", "expert"), axis=0, tiled=True),
        lax.all_gather(router_weight, ("dp", "expert"), axis=0, tiled=True),
    )
    up_full, down_full = (
        lax.all_gather(up_weight, "dp", axis=2, tiled=True),
        lax.all_gather(down_weight, "dp", axis=1, tiled=True),
    )
    key_value = lax.all_gather(packed[:, width:], "dp", axis=0, tiled=True)
    key_blocks, value_blocks = split_blocks(key_value)
    upstream = cotangent[0].astype(jnp.float32)
    d_gate = jnp.sum(upstream * combined, axis=-1)
    table32 = table.astype(jnp.float32)
    d_result = jnp.einsum("tec,td->ecd", table32, gate[:, None] * upstream, precision=HIGH).astype(
        jnp.bfloat16
    )
    d_arrived = lax.all_to_all(d_result, "expert", split_axis=0, concat_axis=0, tiled=True)
    d_rows = d_arrived.reshape(-1, width)
    grad_down_bias = jnp.sum(d_rows.astype(jnp.float32), axis=0)
    grad_down = jnp.einsum("rf,rd->fd", act_low, d_rows, preferred_element_type=jnp.float32)
    d_act = jnp.einsum("rd,fd->rf", d_rows, down_full[0], preferred_element_type=jnp.float32)
    d_pre = act_back(d_act)[0]
    grad_up_bias = jnp.sum(d_pre, axis=0)
    d_pre_low = d_pre.astype(jnp.bfloat16)
    grad_up = jnp.einsum("rd,rf->df", slots, d_pre_low, preferred_element_type=jnp.float32)
    d_slots = jnp.einsum(
        "rf,df->rd", d_pre_low, up_full[0], preferred_element_type=jnp.float32
    ).astype(jnp.bfloat16)
    d_sent = lax.all_to_all(
        d_slots.reshape(arrived.shape), "expert", split_axis=0, concat_axis=0, tiled=True
    )
    d_logits = gate_back(d_gate)[0]
    grad_router = jnp.einsum("td,te->de", normed2_low.astype(jnp.float32), d_logits, precision=HIGH)
    d_normed2 = jnp.einsum("tec,ecd->td", table_low, d_sent, preferred_element_type=jnp.float32)
    d_normed2 = d_normed2 + jnp.einsum(
        "te,de->td", d_logits, router_full.astype(jnp.float32), precision=HIGH
    )
    d_mixed_norm, grad_gain_second, grad_shift_norm2 = norm2_back(d_normed2)
    d_mixed = upstream + d_mixed_norm
    grad_shift_proj = jnp.sum(d_mixed, axis=0)
    d_mixed_low = d_mixed.astype(jnp.bfloat16)
    grad_proj = jnp.einsum(
        "tc,td->cd", attended_low, d_mixed_low, preferred_element_type=jnp.float32
    )
    d_attended = jnp.einsum(
        "td,cd->tc", d_mixed_low, proj_full, preferred_element_type=jnp.float32
    ).astype(jnp.bfloat16)
    d_heads = d_attended.reshape(rows, H, head_dim)
    delta = jnp.einsum("qhd,qhd->hq", d_heads.astype(jnp.float32), attended32, precision=HIGH)

    def grad_step(d_query, item):
        scores = block_scores(item[0], item[1], item[2])
        probs = jnp.exp(scores - log_total[:, :, None])
        probs_low = probs.astype(jnp.bfloat16)
        d_value = jnp.einsum("hqk,qhd->khd", probs_low, d_heads, preferred_element_type=jnp.float32)
        d_probs = jnp.einsum("qhd,khd->hqk", d_heads, item[3], preferred_element_type=jnp.float32)
        d_scores = (probs * (d_probs - delta[:, :, None])).astype(jnp.bfloat16)
        d_query = d_query + jnp.einsum(
            "hqk,khd->qhd", d_scores, item[0], preferred_element_type=jnp.float32
        )
        d_key = (
            jnp.einsum("hqk,qhd->khd", d_scores, query_heads, preferred_element_type=jnp.float32)
            * scale
        )
        joined = jnp.concatenate(
            [d_key.reshape(block, width), d_value.reshape(block, width)], axis=1
        )
        return (d_query, joined)

    d_query, joined = lax.scan(
        grad_step,
        jnp.zeros((rows, H, head_dim), jnp.float32),
        (key_blocks, hot_blocks, pos_blocks, value_blocks),
    )
    joined_rows = joined.reshape(length, 2 * width)
    d_key_value = lax.psum_scatter(
        joined_rows.astype(jnp.bfloat16), "dp", scatter_dimension=0, tiled=True
    ).astype(jnp.float32)
    d_packed = jnp.concatenate(
        [(d_query * scale).reshape(rows, width), d_key_value], axis=1
    ).astype(jnp.bfloat16)
    packed_sums = jnp.sum(d_packed.astype(jnp.float32), axis=0)
    grad_qkv = jnp.einsum("tc,te->ce", normed_low, d_packed, preferred_element_type=jnp.float32)
    d_normed = jnp.einsum("te,ce->tc", d_packed, qkv_full, preferred_element_type=jnp.float32)
    d_inputs, grad_gain_first, grad_shift_norm1 = norm1_back(d_normed)
    grad_tokens = d_mixed + d_inputs
    grad_gains = jnp.stack([grad_gain_first, grad_gain_second])
    grad_biases = jnp.stack(
        [
            grad_shift_norm1,
            packed_sums[:width],
            packed_sums[2 * width :],
            grad_shift_proj,
            grad_shift_norm2,
        ]
    )
    owned_qkv, owned_proj, owned_router, owned_gains, owned_biases = (
        lax.psum_scatter(grad_qkv, ("dp", "expert"), scatter_dimension=0, tiled=True),
        lax.psum_scatter(grad_proj, ("dp", "expert"), scatter_dimension=0, tiled=True),
        lax.psum_scatter(grad_router, ("dp", "expert"), scatter_dimension=0, tiled=True),
        lax.psum_scatter(grad_gains, ("dp", "expert"), scatter_dimension=1, tiled=True),
        lax.psum_scatter(grad_biases, ("dp", "expert"), scatter_dimension=1, tiled=True),
    )
    owned_up, owned_up_bias, owned_down, owned_down_bias = (
        lax.psum_scatter(
            grad_up[None].astype(jnp.bfloat16), "dp", scatter_dimension=2, tiled=True
        ).astype(jnp.float32),
        lax.psum_scatter(
            grad_up_bias[None].astype(jnp.bfloat16), "dp", scatter_dimension=1, tiled=True
        ).astype(jnp.float32),
        lax.psum_scatter(
            grad_down[None].astype(jnp.bfloat16), "dp", scatter_dimension=1, tiled=True
        ).astype(jnp.float32),
        lax.psum_scatter(
            grad_down_bias[None].astype(jnp.bfloat16), "dp", scatter_dimension=1, tiled=True
        ).astype(jnp.float32),
    )
    return (
        outputs[None],
        grad_tokens[None],
        owned_qkv,
        owned_proj,
        owned_router,
        owned_gains,
        owned_biases,
        owned_up,
        owned_up_bias,
        owned_down,
        owned_down_bias,
    )


def solution(mesh):
    placed = (
        P("expert", "dp", None),
        P(("dp", "expert"), None),
        P(("dp", "expert"), None),
        P(("dp", "expert"), None),
        P(None, ("dp", "expert")),
        P(None, ("dp", "expert")),
        P("expert", None, "dp"),
        P("expert", "dp"),
        P("expert", "dp", None),
        P("expert", "dp"),
        P("expert", "dp", None),
        P("expert", "dp", None),
        P("expert", None),
        P("expert", None),
        P("expert", "dp", None),
    )
    return jax.shard_map(
        shards,
        mesh=mesh,
        in_specs=placed,
        out_specs=(
            P("expert", "dp", None),
            P("expert", "dp", None),
            P(("dp", "expert"), None),
            P(("dp", "expert"), None),
            P(("dp", "expert"), None),
            P(None, ("dp", "expert")),
            P(None, ("dp", "expert")),
            P("expert", None, "dp"),
            P("expert", "dp"),
            P("expert", "dp", None),
            P("expert", "dp"),
        ),
        check_vma=False,
    )
```

profile of v0, /device:TPU:0, one launch (start us, length us, event | category | flops | bytes accessed | tf_op | source)
XLA Modules:
  0.0 1658.2 jit_solution(5418637222346388384)
XLA Ops:
  8.0 43.2 %all-gather = bf16[32,32,2]{1,2,0:T(2,128)(2,1)S(1)} all-gather(bf16[1,32,2]{1,2,0:T(2,128)(2,1)} %bitcast.257), channel_id=1, replica_groups=mesh['dp'=4,'expert'=8] {'dp','expert'}, dimensions={0}, use_global_device_ids=true | all-gather | bytes 4224 | tf_op jit(solution)/shard_map/all_gather | solution.py:71
  51.3 37.4 %all-gather.1 = bf16[32,32,5]{1,2,0:T(8,128)(2,1)S(1)} all-gather(bf16[1,32,5]{1,2,0:T(8,128)(2,1)} %bitcast.252), channel_id=1, replica_groups=mesh['dp'=4,'expert'=8] {'dp','expert'}, dimensions={0}, use_global_device_ids=true | all-gather | bytes 10560 | tf_op jit(solution)/shard_map/all_gather | solution.py:72
  91.2 4.0 fusion.12
  99.6 40.3 %all-gather.11.cloned.1.call-done = bf16[512,2048]{1,0:T(8,128)(2,1)} async-done(((bf16[128,2048]{1,0:T(8,128)(2,1)}), bf16[512,2048]{1,0:T(8,128)(2,1)}) %all-gather.11.cloned.1.call-update) | async-done | bytes 2097168 | tf_op jit(solution)/shard_map/all_gather | solution.py:95
  139.9 1.7 fusion.108
  145.7 2.1 bitcast_convert_fusion
  147.7 50.2 %all-gather.13.cloned.1.call-done = bf16[1024,1024]{1,0:T(8,128)(2,1)} async-done(((bf16[32,1024]{1,0:T(8,128)(2,1)}), bf16[1024,1024]{1,0:T(8,128)(2,1)}) %all-gather.13.cloned.1.call-update) | async-done | bytes 2097168 | tf_op jit(solution)/shard_map/all_gather | solution.py:69
  197.9 2.2 fusion.112
  201.5 3.5 all-to-all-start
  205.0 9.8 all_gather.45
  214.8 15.4 all_gather.43
  230.2 41.5 %all-gather.2 = bf16[32,32,8]{1,2,0:T(8,128)(2,1)S(1)} all-gather(bf16[1,32,8]{1,2,0:T(8,128)(2,1)S(1)} %bitcast.255), channel_id=1, replica_groups=mesh['dp'=4,'expert'=8] {'dp','expert'}, dimensions={0}, use_global_device_ids=true | all-gather | bytes 16896 | tf_op jit(solution)/shard_map/all_gather | solution.py:70
  272.2 76.2 %all-gather.15.cloned.1.call-done = bf16[1,1024,4096]{2,1,0:T(8,128)(2,1)} async-done(((bf16[1,1024,1024]{2,1,0:T(8,128)(2,1)}), bf16[1,1024,4096]{2,1,0:T(8,128)(2,1)}) %all-gather.15.cloned.1.call-update) | async-done | bytes 8388624 | tf_op jit(solution)/shard_map/all_gather | solution.py:75
  348.4 6.2 fusion.8
  354.6 143.1 %all-gather.17.cloned.1.call-done = bf16[1,4096,1024]{2,1,0:T(8,128)(2,1)} async-done(((bf16[1,1024,1024]{2,1,0:T(8,128)(2,1)}), bf16[1,4096,1024]{2,1,0:T(8,128)(2,1)}) %all-gather.17.cloned.1.call-update) | async-done | bytes 8388624 | tf_op jit(solution)/shard_map/all_gather | solution.py:77
  497.7 5.8 fusion.26
  504.4 3.7 all-to-all-start.1
  508.1 8.3 all-to-all-done.1
  517.4 10.7 all_to_all.20
  528.2 8.0 fusion.114
  537.4 6.3 fusion.29
  544.5 3.5 all-to-all-start.3
  548.2 8.0 all-to-all-done.3
  560.1 3.6 convolution_convert_fusion
  563.8 1.7 multiply_convert_fusion
  567.0 2.4 copy.70
  569.5 2.3 fusion.99
  574.0 1.6 reshape_bitcast_fusion
  575.6 1.5 fusion.32
  577.1 32.7 %reduce-scatter.31.cloned.1.call-done = bf16[128,2048]{1,0:T(8,128)(2,1)} async-done(((bf16[512,2048]{1,0:T(8,128)(2,1)}), bf16[128,2048]{1,0:T(8,128)(2,1)}) %reduce-scatter.31.cloned.1.call-update) | async-done | bytes 524304
  612.4 5.2 fusion.106
  621.4 7.3 convert_bitcast_fusion
  630.1 5.7 convert_bitcast_fusion.1
  636.7 2.7 fusion.62
  640.4 6.5 fusion.56
  647.0 98.7 %reduce-scatter.33.cloned.1.call-done = f32[32,8]{1,0:T(8,128)} async-done(((f32[1024,8]{1,0:T(8,128)}), f32[32,8]{1,0:T(8,128)}) %reduce-scatter.33.cloned.1.call-update) | async-done | bytes 1040
  745.6 1.4 copy.73
  747.0 16.5 reduce-scatter.41.cloned.1.call-done
  765.0 26.3 %reduce-scatter.39.cloned.1.call-done = bf16[1024,1]{1,0:T(8,128)(2,1)} async-done(((bf16[4096,1]{1,0:T(8,128)(2,1)}), bf16[1024,1]{1,0:T(8,128)(2,1)}) %reduce-scatter.39.cloned.1.call-update) | async-done | bytes 2064
  793.0 133.7 %reduce-scatter.35.cloned.1.call-done = f32[32,2]{1,0:T(8,128)} async-done(((f32[1024,2]{1,0:T(8,128)}), f32[32,2]{1,0:T(8,128)}) %reduce-scatter.35.cloned.1.call-update) | async-done | bytes 272
  928.0 130.7 %reduce-scatter.37.cloned.1.call-done = f32[32,5]{1,0:T(8,128)} async-done(((f32[1024,5]{1,0:T(8,128)}), f32[32,5]{1,0:T(8,128)}) %reduce-scatter.37.cloned.1.call-update) | async-done | bytes 656
  1058.7 1.4 copy.77
  1060.0 141.2 %reduce-scatter.29.cloned.1.call-done = bf16[1,1024,1024]{2,1,0:T(8,128)(2,1)} async-done(((bf16[1,4096,1024]{2,1,0:T(8,128)(2,1)}), bf16[1,1024,1024]{2,1,0:T(8,128)(2,1)}) %reduce-scatter.29.cloned.1.call-update) | async-done | bytes 2097168 | tf_op jit(solution)/shard_map/reduce_scatter | solution.py:292
  1201.3 4.1 convert_element_type.182
  1205.3 143.5 %reduce-scatter.27.cloned.1.call-done = bf16[1,1024,1024]{2,1,0:T(8,128)(2,1)} async-done(((bf16[1,1024,4096]{2,1,0:T(8,128)(2,1)}), bf16[1,1024,1024]{2,1,0:T(8,128)(2,1)}) %reduce-scatter.27.cloned.1.call-update) | async-done | bytes 2097168 | tf_op jit(solution)/shard_map/reduce_scatter | solution.py:286
  1348.9 4.1 convert_element_type.176
  1352.9 140.4 %reduce-scatter.25.cloned.1.call-done = f32[32,1024]{1,0:T(8,128)} async-done(((f32[1024,1024]{1,0:T(8,128)}), f32[32,1024]{1,0:T(8,128)}) %reduce-scatter.25.cloned.1.call-update) | async-done | bytes 131088 | tf_op jit(solution)/shard_map/reduce_scatter | solution.py:280
  1493.3 158.1 %reduce-scatter.23.cloned.1.call-done = f32[32,3072]{1,0:T(8,128)} async-done(((f32[1024,3072]{1,0:T(8,128)}), f32[32,3072]{1,0:T(8,128)}) %reduce-scatter.23.cloned.1.call-update) | async-done | bytes 393232 | tf_op jit(solution)/shard_map/reduce_scatter | solution.py:279
  (177 shorter events, 39.2 us)
Async XLA Ops:
  7.2 84.0 %all-gather.9.cloned.1.call-start = ((), (), s32[]{:S(2)}) async-start(), calls=%async_computation.14 | async-start | bytes 6488064 | tf_op jit(solution)/shard_map/all_gather | solution.py:68
  7.9 132.0 %all-gather.11.cloned.1.call-start = ((), (), s32[]{:S(2)}) async-start(), calls=%async_computation.15 | async-start | bytes 2621440 | tf_op jit(solution)/shard_map/all_gather | solution.py:95
  96.0 2.0 copy-start.26
  96.0 2.0 copy-start.30
  96.0 2.2 copy-start.32
  96.0 2.7 copy-start.28
  96.0 101.9 %all-gather.13.cloned.1.call-start = ((), (), s32[]{:S(2)}) async-start(), calls=%async_computation.16 | async-start | bytes 2162688 | tf_op jit(solution)/shard_map/all_gather | solution.py:69
  96.7 251.7 %all-gather.15.cloned.1.call-start = ((), (), s32[]{:S(2)}) async-start(), calls=%async_computation.17 | async-start | bytes 10485760 | tf_op jit(solution)/shard_map/all_gather | solution.py:75
  97.3 400.4 %all-gather.17.cloned.1.call-start = ((), (), s32[]{:S(2)}) async-start(), calls=%async_computation.18 | async-start | bytes 10485760 | tf_op jit(solution)/shard_map/all_gather | solution.py:77
  99.6 43.1 %copy-start.17 = (bf16[128,1024]{0,1:T(8,128)(2,1)}, bf16[128,1024]{0,1:T(8,128)(2,1)S(1)}, u32[]{:S(2)}) copy-start(bf16[128,1024]{0,1:T(8,128)(2,1)S(1)} %copy.58) | copy-start | bytes 786436
  142.7 2.2 copy-start.19
  143.6 2.0 copy-start
  145.7 52.2 %copy-start.2 = (bf16[1,128,1024]{2,1,0:T(8,128)(2,1)S(1)}, bf16[1,128,1024]{2,1,0:T(8,128)(2,1)}, u32[]{:S(2)}) copy-start(bf16[1,128,1024]{2,1,0:T(8,128)(2,1)} %param.15) | copy-start | bytes 786436
  147.7 52.6 %copy-start.21 = (bf16[128,16,64]{0,2,1:T(8,128)(2,1)}, bf16[128,16,64]{0,2,1:T(8,128)(2,1)S(1)}, u32[]{:S(2)}) copy-start(bf16[128,16,64]{0,2,1:T(8,128)(2,1)S(1)} %get-tuple-element.134) | copy-start | bytes 786436
  197.9 7.1 copy-start.31
  197.9 16.9 %copy-start.27 = (bf16[1,1024]{1,0:T(2,128)(2,1)S(1)}, bf16[1,1024]{1,0:T(2,128)(2,1)}, u32[]{:S(2)}) copy-start(bf16[1,1024]{1,0:T(2,128)(2,1)} %param.22) | copy-start | bytes 6148
  197.9 32.3 %copy-start.29 = (bf16[32,8]{0,1:T(8,128)(2,1)S(1)}, bf16[32,8]{0,1:T(8,128)(2,1)}, u32[]{:S(2)}) copy-start(bf16[32,8]{0,1:T(8,128)(2,1)} %param.18) | copy-start | bytes 1540
  200.5 154.1 %copy-start.12 = (bf16[128,1024]{1,0:T(8,128)(2,1)}, bf16[128,1024]{1,0:T(8,128)(2,1)S(1)}, u32[]{:S(2)}) copy-start(bf16[128,1024]{1,0:T(8,128)(2,1)S(1)} %add_convert_fusion.1) | copy-start | bytes 786436
  201.5 70.5 %all-to-all-start = ((bf16[8,18,1024]{2,1,0:T(8,128)(2,1)}), bf16[8,18,1024]{2,1,0:T(8,128)(2,1)S(1)}, u32[]{:S(2)}, u32[]{:S(2)}) async-start(bf16[8,18,1024]{2,1,0:T(8,128)(2,1)} %convolution_convert_fusion.2), calls=%async_computation | async-start | bytes 786432 | tf_op jit(solution)/shard_map/all_to_all | solution.py:165
  272.1 82.4 %copy-start.13 = (bf16[144,1024]{1,0:T(8,128)(2,1)}, bf16[144,1024]{1,0:T(8,128)(2,1)S(1)}, u32[]{:S(2)}) copy-start(bf16[144,1024]{1,0:T(8,128)(2,1)S(1)} %reshape.239) | copy-start | bytes 884740
  497.7 18.7 %copy-start.8 = (bf16[1,128,1024]{2,1,0:T(8,128)(2,1)S(1)}, bf16[1,128,1024]{2,1,0:T(8,128)(2,1)}, u32[]{:S(2)}) copy-start(bf16[1,128,1024]{2,1,0:T(8,128)(2,1)} %param.29) | copy-start | bytes 786436
  504.4 12.0 all-to-all-start.1
  528.1 8.1 copy-start.15
  528.2 8.0 copy-start.24
  536.3 1.1 copy-start.10
  544.5 11.7 all-to-all-start.3
  548.0 61.9 %reduce-scatter.31.cloned.1.call-start = ((), (), s32[]{:S(2)}) async-start(), calls=%async_computation.23 | async-start | bytes 2621440
  556.2 2.7 copy-start.3
  558.2 1.8 copy-start.23
  560.1 3.6 copy-start.1
  560.1 3.7 copy-start.20
  563.8 1.7 copy-start.18
  565.5 1.4 copy-start.4
  569.4 6.2 copy-start.5
  569.4 176.2 %reduce-scatter.33.cloned.1.call-start = ((), (), s32[]{:S(2)}) async-start(), calls=%async_computation.24 | async-start | bytes 540672
  571.8 191.7 %reduce-scatter.41.cloned.1.call-start = ((), (), s32[]{:S(2)}) async-start(), calls=%async_computation.28 | async-start | bytes 327680
  573.9 217.4 %reduce-scatter.39.cloned.1.call-start = ((), (), s32[]{:S(2)}) async-start(), calls=%async_computation.27 | async-start | bytes 1310720
  575.6 351.1 %reduce-scatter.35.cloned.1.call-start = ((), (), s32[]{:S(2)}) async-start(), calls=%async_computation.25 | async-start | bytes 540672
  612.4 6.8 copy-start.7
  612.4 6.8 copy-start.9
  618.0 3.4 copy-start.25
  619.1 439.5 %reduce-scatter.37.cloned.1.call-start = ((), (), s32[]{:S(2)}) async-start(), calls=%async_computation.26 | async-start | bytes 540672
  621.4 579.9 %reduce-scatter.29.cloned.1.call-start = ((), (), s32[]{:S(2)}) async-start(), calls=%async_computation.22 | async-start | bytes 10485760 | tf_op jit(solution)/shard_map/reduce_scatter | solution.py:292
  628.8 1.3 copy-start.11
  628.8 1.3 copy-start.14
  628.8 720.1 %reduce-scatter.27.cloned.1.call-start = ((), (), s32[]{:S(2)}) async-start(), calls=%async_computation.21 | async-start | bytes 10485760 | tf_op jit(solution)/shard_map/reduce_scatter | solution.py:286
  635.8 857.5 %reduce-scatter.25.cloned.1.call-start = ((), (), s32[]{:S(2)}) async-start(), calls=%async_computation.20 | async-start | bytes 4325376 | tf_op jit(solution)/shard_map/reduce_scatter | solution.py:280
  639.5 1011.9 %reduce-scatter.23.cloned.1.call-start = ((), (), s32[]{:S(2)}) async-start(), calls=%async_computation.19 | async-start | bytes 12976128 | tf_op jit(solution)/shard_map/reduce_scatter | solution.py:279
  (3 other events, 2.7 us)
Sparse Core Ops, SparseCore 0:
  10.9 71.9 all-gather.8
  96.1 43.7 all-gather.10
  142.8 55.0 all-gather.12
  199.3 149.0 all-gather.14
  349.8 147.8 all-gather.16
  569.5 40.3 reduce-scatter.30
  612.2 133.3 reduce-scatter.32
  747.9 15.5 reduce-scatter.40
  765.9 25.3 reduce-scatter.38
  793.9 132.6 reduce-scatter.34
  929.0 129.6 reduce-scatter.36
  1060.9 140.3 reduce-scatter.28
  1203.6 145.1 reduce-scatter.26
  1351.6 141.6 reduce-scatter.24
  1499.7 151.6 reduce-scatter.22
where the time goes:
time: 1670 us; the launch traced here: 1660 us
  waiting for transfers between devices  1350 us (81%)
  blocking collectives  158 us (9%)
  matrix products  77.5 us (5%)
  local copies, waits for them, and re-layouts  27.1 us (2%)
  other arithmetic  18.6 us (1%)
    unnamed x21, waiting for transfers between devices  441 us
    reduce_scatter x1, waiting for transfers between devices, shards(): lax.psum_scatter(grad_qkv, ('dp', 'expert'), scatter_dimension=0, tiled=T...  158 us
    reduce_scatter x1, waiting for transfers between devices, shards(): lax.psum_scatter(grad_up[None].astype(jnp.bfloat16), 'dp', scatter_dimens...  144 us
    all_gather x1, waiting for transfers between devices, shards(): lax.all_gather(down_weight, 'dp', axis=1, tiled=True)  143 us
    reduce_scatter x1, waiting for transfers between devices, shards(): lax.psum_scatter(grad_down[None].astype(jnp.bfloat16), 'dp', scatter_dime...  141 us
    reduce_scatter x1, waiting for transfers between devices, shards(): lax.psum_scatter(grad_proj, ('dp', 'expert'), scatter_dimension=0, tiled=...  140 us
    all_gather x1, waiting for transfers between devices, shards(): lax.all_gather(up_weight, 'dp', axis=2, tiled=True)  76.2 us
    all_gather x1, waiting for transfers between devices, shards(): lax.all_gather(proj_weight, ('dp', 'expert'), axis=0, tiled=True)  50.2 us
  transfers between devices with their start and end apart: 18, of which 16 were waited for; matrix products, arithmetic and copies ran while one was open for 5% of the time, Pallas kernels for 0%

commit v1 on v0

--- a/solution.py
+++ b/solution.py
@@ -10,6 +10,35 @@
 EPS = 1e-05
 NEG = -1e30
 HIGH = lax.Precision.HIGHEST
+
+
+def _launch_waves(z_in, on_dim):
+    item_now = lax.axis_size("dp")
+    next_value = lax.axis_index("dp")
+    high, local_out, back = (item_now, next_value, z_in.shape[on_dim])
+    all_rows = []
+    for w in range(high):
+        all_rows.append((w, (w + 1) % high))
+    store = []
+    for w in range(high):
+        store.append((w, (w - 1) % high))
+    part_next = jnp.zeros(
+        (*z_in.shape[:on_dim], high * back, *z_in.shape[on_dim + 1 :]), z_in.dtype
+    )
+    spare = then = z_in
+    part_next = lax.dynamic_update_slice_in_dim(part_next, z_in, local_out * back, axis=on_dim)
+    near = high // 2
+    for dd in range(1, near + 1):
+        spare = lax.ppermute(spare, axis_name="dp", perm=all_rows)
+        part_next = lax.dynamic_update_slice_in_dim(
+            part_next, spare, (local_out - dd) % high * back, axis=on_dim
+        )
+        if dd < high - near:
+            then = lax.ppermute(then, perm=store, axis_name="dp")
+            part_next = lax.dynamic_update_slice_in_dim(
+                part_next, then, (local_out + dd) % high * back, axis=on_dim
+            )
+    return part_next
 
 
 def layer_norm(values, gain, shift):
@@ -72,7 +101,7 @@
         lax.all_gather(biases, ("dp", "expert"), axis=1, tiled=True),
     )
     up_full, up_shift, down_full, down_shift = (
-        lax.all_gather(up_weight, "dp", axis=2, tiled=True),
+        _launch_waves(up_weight, 2),
         lax.all_gather(up_bias, "dp", axis=1, tiled=True),
         lax.all_gather(down_weight, "dp", axis=1, tiled=True),
         lax.all_gather(down_bias, "dp", axis=1, tiled=True),

time: 1670 us -> 1740 us (1.042)
  blocking collectives: 158 us -> 271 us
  waiting for transfers between devices: 1350 us -> 1280 us
  local copies, waits for them, and re-layouts: 27.1 us -> 45.2 us
    all_gather x1, blocking collectives: 15.4 us -> 133 us  [shards(): lax.all_gather(up_bias, 'dp', axis=1, tiled=True)]
    all_gather x1, waiting for transfers between devices: 143 us -> 62.8 us  [shards(): lax.all_gather(down_weight, 'dp', axis=1, tiled=True)]
    ppermute x0 -> x3, waiting for transfers between devices: none -> 69.5 us  [the longest x2 69.5 us: _launch_waves(): spare = lax.ppermute(spare, axis_name='dp', perm=all_rows)]
    all_gather x1, waiting for transfers between devices: 50.2 us -> 0.02 us  [shards(): lax.all_gather(proj_weight, ('dp', 'expert'), axis=0, tiled=True)]
    all_gather x1, waiting for transfers between devices: 40.3 us -> 0.02 us  [shards(): key_value = lax.all_gather(packed[:, width:], 'dp', axis=0, tiled=True)]
    all_gather x1, waiting for transfers between devices: 76.2 us -> 109 us  [shards(): lax.all_gather(up_weight, 'dp', axis=2, tiled=True)]
  transfers between devices with their start and end apart: 18 -> 21, of which waited for: 16 -> 15; matrix products, arithmetic and copies ran while one was open for 5% -> 7% of each run, Pallas kernels for 0% -> 0%
where the time goes in v1:
time: 1740 us; the launch traced here: 1730 us
  waiting for transfers between devices  1280 us (74%)
  blocking collectives  271 us (16%)
  matrix products  81.5 us (5%)
  local copies, waits for them, and re-layouts  45.2 us (3%)
  other arithmetic  19.2 us (1%)
    unnamed x21, waiting for transfers between devices  441 us
    reduce_scatter x1, waiting for transfers between devices, shards(): lax.psum_scatter(grad_qkv, ('dp', 'expert'), scatter_dimension=0, tiled=T...  158 us
    reduce_scatter x1, waiting for transfers between devices, shards(): lax.psum_scatter(grad_up[None].astype(jnp.bfloat16), 'dp', scatter_dimens...  143 us
    reduce_scatter x1, waiting for transfers between devices, shards(): lax.psum_scatter(grad_down[None].astype(jnp.bfloat16), 'dp', scatter_dime...  141 us
    reduce_scatter x1, waiting for transfers between devices, shards(): lax.psum_scatter(grad_proj, ('dp', 'expert'), scatter_dimension=0, tiled=...  140 us
    all_gather x1, blocking collectives, shards(): lax.all_gather(up_bias, 'dp', axis=1, tiled=True)  133 us
    all_gather x1, waiting for transfers between devices, shards(): lax.all_gather(up_weight, 'dp', axis=2, tiled=True)  109 us
    ppermute x2, waiting for transfers between devices, _launch_waves(): spare = lax.ppermute(spare, axis_name='dp', perm=all_rows)  69.5 us
  transfers between devices with their start and end apart: 21, of which 15 were waited for; matrix products, arithmetic and copies ran while one was open for 7% of the time, Pallas kernels for 0%

profile of v1, /device:TPU:0, one launch (start us, length us, event | category | flops | bytes accessed | tf_op | source)
XLA Modules:
  0.0 1729.1 jit_solution(5984895198949414510)
XLA Ops:
  8.0 43.9 %all-gather.1 = bf16[32,32,5]{1,2,0:T(8,128)(2,1)S(1)} all-gather(bf16[1,32,5]{1,2,0:T(8,128)(2,1)} %bitcast.257), channel_id=1, replica_groups=mesh['dp'=4,'expert'=8] {'dp','expert'}, dimensions={0}, use_global_device_ids=true | all-gather | bytes 10560 | tf_op jit(solution)/shard_map/all_gather | solution.py:101
  51.9 36.8 %all-gather = bf16[32,32,2]{1,2,0:T(2,128)(2,1)S(1)} all-gather(bf16[1,32,2]{1,2,0:T(2,128)(2,1)} %bitcast.262), channel_id=1, replica_groups=mesh['dp'=4,'expert'=8] {'dp','expert'}, dimensions={0}, use_global_device_ids=true | all-gather | bytes 4224 | tf_op jit(solution)/shard_map/all_gather | solution.py:100
  91.1 4.0 fusion.7
  98.0 3.8 collective-permute-start.1
  101.8 133.0 %all_gather.41 = bf16[1,4096]{1,0:T(2,128)(2,1)S(1)} all-gather(bf16[1,1024]{1,0:T(2,128)(2,1)S(1)} %copy-done.31), channel_id=1, replica_groups=mesh['dp'=4,'expert'=8] {'dp'}, dimensions={1}, use_global_device_ids=true | all-gather | bytes 10240 | tf_op jit(solution)/shard_map/all_gather | solution.py:105
  234.9 7.9 all_gather.43
  243.5 38.3 %all-gather.2 = bf16[32,32,8]{1,2,0:T(8,128)(2,1)S(1)} all-gather(bf16[1,32,8]{1,2,0:T(8,128)(2,1)S(1)} %bitcast.258), channel_id=1, replica_groups=mesh['dp'=4,'expert'=8] {'dp','expert'}, dimensions={0}, use_global_device_ids=true | all-gather | bytes 16896 | tf_op jit(solution)/shard_map/all_gather | solution.py:99
  283.4 4.3 squeeze.58
  289.3 3.2 bitcast_dynamic-update-slice_fusion.2
  292.5 3.2 bitcast_dynamic-update-slice_fusion.1
  299.2 2.0 copy-done
  303.0 4.6 bitcast_convert_fusion
  307.6 2.2 fusion.107
  311.3 3.9 all-to-all-start
  315.2 69.5 %collective-permute-done.2 = bf16[1,1024,1024]{2,1,0:T(8,128)(2,1)} collective-permute-done((bf16[1,1024,1024]{2,1,0:T(8,128)(2,1)}, bf16[1,1024,1024]{2,1,0:T(8,128)(2,1)}, u32[]{:S(2)}, u32[]{:S(2)}) %collective-permute-start.2) | collective-permute-done | bytes 2097184 | tf_op jit(solution)/shard_map/ppermute | solution.py:32
  384.7 3.1 bitcast_dynamic-update-slice_fusion
  388.1 6.3 convolution_add_fusion
  394.4 62.8 %all-gather.15.cloned.1.call-done = bf16[1,4096,1024]{2,1,0:T(8,128)(2,1)} async-done(((bf16[1,1024,1024]{2,1,0:T(8,128)(2,1)}), bf16[1,4096,1024]{2,1,0:T(8,128)(2,1)}) %all-gather.15.cloned.1.call-update) | async-done | bytes 8388624 | tf_op jit(solution)/shard_map/all_gather | solution.py:106
  457.3 5.8 fusion.21
  463.9 3.7 all-to-all-start.1
  467.6 8.3 all-to-all-done.1
  477.7 10.7 all_to_all.20
  490.0 8.0 fusion.109
  498.0 108.6 %all-gather.17.cloned.1.call-done = bf16[1,1024,4096]{2,1,0:T(8,128)(2,1)} async-done(((bf16[1,1024,1024]{2,1,0:T(8,128)(2,1)}), bf16[1,1024,4096]{2,1,0:T(8,128)(2,1)}) %all-gather.17.cloned.1.call-update) | async-done | bytes 8388624 | tf_op jit(solution)/shard_map/all_gather | solution.py:216
  606.6 7.0 fusion.24
  613.5 1.8 reshape.250
  615.3 3.8 all-to-all-start.3
  619.4 8.1 all-to-all-done.3
  631.4 3.6 convolution_convert_fusion
  638.3 2.4 copy.70
  640.7 2.3 fusion.94
  648.4 32.7 %reduce-scatter.31.cloned.1.call-done = bf16[128,2048]{1,0:T(8,128)(2,1)} async-done(((bf16[512,2048]{1,0:T(8,128)(2,1)}), bf16[128,2048]{1,0:T(8,128)(2,1)}) %reduce-scatter.31.cloned.1.call-update) | async-done | bytes 524304
  683.7 5.2 fusion.101
  692.7 7.3 convert_bitcast_fusion
  701.3 5.7 convert_bitcast_fusion.1
  707.9 2.7 fusion.57
  711.6 6.5 fusion.51
  718.1 98.7 %reduce-scatter.33.cloned.1.call-done = f32[32,8]{1,0:T(8,128)} async-done(((f32[1024,8]{1,0:T(8,128)}), f32[32,8]{1,0:T(8,128)}) %reduce-scatter.33.cloned.1.call-update) | async-done | bytes 1040
  818.2 16.5 reduce-scatter.41.cloned.1.call-done
  836.2 26.3 %reduce-scatter.39.cloned.1.call-done = bf16[1024,1]{1,0:T(8,128)(2,1)} async-done(((bf16[4096,1]{1,0:T(8,128)(2,1)}), bf16[1024,1]{1,0:T(8,128)(2,1)}) %reduce-scatter.39.cloned.1.call-update) | async-done | bytes 2064
  864.2 133.4 %reduce-scatter.35.cloned.1.call-done = f32[32,2]{1,0:T(8,128)} async-done(((f32[1024,2]{1,0:T(8,128)}), f32[32,2]{1,0:T(8,128)}) %reduce-scatter.35.cloned.1.call-update) | async-done | bytes 272
  999.0 131.0 %reduce-scatter.37.cloned.1.call-done = f32[32,5]{1,0:T(8,128)} async-done(((f32[1024,5]{1,0:T(8,128)}), f32[32,5]{1,0:T(8,128)}) %reduce-scatter.37.cloned.1.call-update) | async-done | bytes 656
  1131.3 141.2 %reduce-scatter.29.cloned.1.call-done = bf16[1,1024,1024]{2,1,0:T(8,128)(2,1)} async-done(((bf16[1,4096,1024]{2,1,0:T(8,128)(2,1)}), bf16[1,1024,1024]{2,1,0:T(8,128)(2,1)}) %reduce-scatter.29.cloned.1.call-update) | async-done | bytes 2097168 | tf_op jit(solution)/shard_map/reduce_scatter | solution.py:321
  1272.5 4.1 convert_element_type.182
  1276.6 143.5 %reduce-scatter.27.cloned.1.call-done = bf16[1,1024,1024]{2,1,0:T(8,128)(2,1)} async-done(((bf16[1,1024,4096]{2,1,0:T(8,128)(2,1)}), bf16[1,1024,1024]{2,1,0:T(8,128)(2,1)}) %reduce-scatter.27.cloned.1.call-update) | async-done | bytes 2097168 | tf_op jit(solution)/shard_map/reduce_scatter | solution.py:315
  1420.1 4.1 convert_element_type.176
  1424.2 140.4 %reduce-scatter.25.cloned.1.call-done = f32[32,1024]{1,0:T(8,128)} async-done(((f32[1024,1024]{1,0:T(8,128)}), f32[32,1024]{1,0:T(8,128)}) %reduce-scatter.25.cloned.1.call-update) | async-done | bytes 131088 | tf_op jit(solution)/shard_map/reduce_scatter | solution.py:309
  1564.6 157.7 %reduce-scatter.23.cloned.1.call-done = f32[32,3072]{1,0:T(8,128)} async-done(((f32[1024,3072]{1,0:T(8,128)}), f32[32,3072]{1,0:T(8,128)}) %reduce-scatter.23.cloned.1.call-update) | async-done | bytes 393232 | tf_op jit(solution)/shard_map/reduce_scatter | solution.py:308
  (206 shorter events, 50.4 us)
Async XLA Ops:
  7.2 84.0 %all-gather.9.cloned.1.call-start = ((), (), s32[]{:S(2)}) async-start(), calls=%async_computation.14 | async-start | bytes 6488064 | tf_op jit(solution)/shard_map/all_gather | solution.py:97
  7.9 288.0 %all-gather.11.cloned.1.call-start = ((), (), s32[]{:S(2)}) async-start(), calls=%async_computation.15 | async-start | bytes 2621440 | tf_op jit(solution)/shard_map/all_gather | solution.py:124
  91.1 4.0 copy-start.39
  96.0 5.9 copy-start.31
  96.0 138.9 %copy-start.38 = (bf16[1,256]{1,0:T(2,128)(2,1)S(1)}, bf16[1,256]{1,0:T(2,128)(2,1)}, u32[]{:S(2)}) copy-start(bf16[1,256]{1,0:T(2,128)(2,1)} %param.24) | copy-start | bytes 1540
  96.0 147.5 %copy-start.35 = (bf16[32,8]{0,1:T(8,128)(2,1)S(1)}, bf16[32,8]{0,1:T(8,128)(2,1)}, u32[]{:S(2)}) copy-start(bf16[32,8]{0,1:T(8,128)(2,1)} %param.18) | copy-start | bytes 1540
  96.0 185.9 %copy-start.27 = (s32[1,128,1]{1,2,0:T(1,128)S(1)}, s32[1,128,1]{1,2,0:T(1,128)}, u32[]{:S(2)}) copy-start(s32[1,128,1]{1,2,0:T(1,128)} %param.25) | copy-start | bytes 1540
  96.0 185.9 %copy-start.37 = (s32[1,1,128]{2,1,0:T(1,128)S(1)}, s32[1,1,128]{2,1,0:T(1,128)}, u32[]{:S(2)}) copy-start(s32[1,1,128]{2,1,0:T(1,128)} %param.26) | copy-start | bytes 1540
  96.0 186.1 %copy-start.41 = (s32[1,7]{1,0:T(1,128)S(1)}, s32[1,7]{1,0:T(1,128)}, u32[]{:S(2)}) copy-start(s32[1,7]{1,0:T(1,128)} %param.28) | copy-start | bytes 88
  96.0 211.6 %all-gather.13.cloned.1.call-start = ((), (), s32[]{:S(2)}) async-start(), calls=%async_computation.16 | async-start | bytes 2162688 | tf_op jit(solution)/shard_map/all_gather | solution.py:98
  96.8 185.9 %copy-start.36 = (s32[1,512]{1,0:T(1,128)S(1)}, s32[1,512]{1,0:T(1,128)}, u32[]{:S(2)}) copy-start(s32[1,512]{1,0:T(1,128)} %param.27) | copy-start | bytes 6148
  96.8 360.5 %all-gather.15.cloned.1.call-start = ((), (), s32[]{:S(2)}) async-start(), calls=%async_computation.17 | async-start | bytes 10485760 | tf_op jit(solution)/shard_map/all_gather | solution.py:106
  97.4 509.2 %all-gather.17.cloned.1.call-start = ((), (), s32[]{:S(2)}) async-start(), calls=%async_computation.18 | async-start | bytes 10485760 | tf_op jit(solution)/shard_map/all_gather | solution.py:216
  98.0 191.3 %collective-permute-start = (bf16[1,1024,1024]{2,1,0:T(8,128)(2,1)S(1)}, bf16[1,1024,1024]{2,1,0:T(8,128)(2,1)}, u32[]{:S(2)}, u32[]{:S(2)}) collective-permute-start(bf16[1,1024,1024]{2,1,0:T(8,128)(2,1)S(1)} %copy-done.3), channel_id=1, source_target_pairs={{0,8},{8,16},{16,24},{24,0},{1,9},{9,17},{17,25},{25,1},{2,10},{10... | collective-permute-start | bytes 6291464 | tf_op jit(solution)/shard_map/ppermute | solution.py:32
  98.0 194.4 %collective-permute-start.1 = (bf16[1,1024,1024]{2,1,0:T(8,128)(2,1)S(1)}, bf16[1,1024,1024]{2,1,0:T(8,128)(2,1)}, u32[]{:S(2)}, u32[]{:S(2)}) collective-permute-start(bf16[1,1024,1024]{2,1,0:T(8,128)(2,1)S(1)} %copy-done.3), channel_id=1, source_target_pairs={{0,24},{8,0},{16,8},{24,16},{1,25},{9,1},{17,9},{25,17},{2,26},{10... | collective-permute-start | bytes 6291464 | tf_op jit(solution)/shard_map/ppermute | solution.py:37
  289.3 95.4 %collective-permute-start.2 = (bf16[1,1024,1024]{2,1,0:T(8,128)(2,1)}, bf16[1,1024,1024]{2,1,0:T(8,128)(2,1)}, u32[]{:S(2)}, u32[]{:S(2)}) collective-permute-start(bf16[1,1024,1024]{2,1,0:T(8,128)(2,1)} %collective-permute-done), channel_id=1, source_target_pairs={{0,8},{8,16},{16,24},{24,0},{1,9},{9,17},{17,25},{25,1},{2,10},{10... | collective-permute-start | bytes 6291464 | tf_op jit(solution)/shard_map/ppermute | solution.py:32
  303.0 4.6 copy-start.21
  303.0 4.6 copy-start.29
  303.0 4.6 copy-start.2
  310.3 77.5 %copy-start.13 = (bf16[128,1024]{1,0:T(8,128)(2,1)}, bf16[128,1024]{1,0:T(8,128)(2,1)S(1)}, u32[]{:S(2)}) copy-start(bf16[128,1024]{1,0:T(8,128)(2,1)S(1)} %add_convert_fusion.1) | copy-start | bytes 786436
  311.3 76.7 %all-to-all-start = ((bf16[8,18,1024]{2,1,0:T(8,128)(2,1)}), bf16[8,18,1024]{2,1,0:T(8,128)(2,1)S(1)}, u32[]{:S(2)}, u32[]{:S(2)}) async-start(bf16[8,18,1024]{2,1,0:T(8,128)(2,1)} %convolution_convert_fusion.2), calls=%async_computation | async-start | bytes 786432 | tf_op jit(solution)/shard_map/all_to_all | solution.py:194
  388.1 6.3 copy-start.14
  388.1 69.2 %copy-start.32 = (f32[1,1024]{1,0:T(1,128)S(1)}, f32[1,1024]{1,0:T(1,128)}, u32[]{:S(2)}) copy-start(f32[1,1024]{1,0:T(1,128)} %add.237) | copy-start | bytes 12292
  457.3 18.7 %copy-start.9 = (bf16[1,128,1024]{2,1,0:T(8,128)(2,1)S(1)}, bf16[1,128,1024]{2,1,0:T(8,128)(2,1)}, u32[]{:S(2)}) copy-start(bf16[1,128,1024]{2,1,0:T(8,128)(2,1)} %param.29) | copy-start | bytes 786436
  463.1 14.0 copy-start.28
  463.9 12.0 all-to-all-start.1
  498.0 115.6 %copy-start.11 = (bf16[144,4096]{1,0:T(8,128)(2,1)}, bf16[144,4096]{1,0:T(8,128)(2,1)S(1)}, u32[]{:S(2)}) copy-start(bf16[144,4096]{1,0:T(8,128)(2,1)S(1)} %get-tuple-element.145) | copy-start | bytes 3538948
  615.3 13.1 copy-start.20
  615.3 12.1 all-to-all-start.3
  619.1 61.9 %reduce-scatter.31.cloned.1.call-start = ((), (), s32[]{:S(2)}) async-start(), calls=%async_computation.23 | async-start | bytes 2621440
  619.4 10.0 copy-start.33
  627.5 2.7 copy-start.4
  631.3 3.6 copy-start.1
  631.3 3.7 copy-start.22
  640.7 6.2 copy-start.6
  640.7 176.1 %reduce-scatter.33.cloned.1.call-start = ((), (), s32[]{:S(2)}) async-start(), calls=%async_computation.24 | async-start | bytes 540672
  643.1 191.6 %reduce-scatter.41.cloned.1.call-start = ((), (), s32[]{:S(2)}) async-start(), calls=%async_computation.28 | async-start | bytes 327680
  645.2 217.3 %reduce-scatter.39.cloned.1.call-start = ((), (), s32[]{:S(2)}) async-start(), calls=%async_computation.27 | async-start | bytes 1310720
  646.8 350.8 %reduce-scatter.35.cloned.1.call-start = ((), (), s32[]{:S(2)}) async-start(), calls=%async_computation.25 | async-start | bytes 540672
  683.6 5.3 copy-start.40
  683.7 6.8 copy-start.8
  683.7 6.8 copy-start.10
  689.3 3.4 copy-start.26
  690.4 439.6 %reduce-scatter.37.cloned.1.call-start = ((), (), s32[]{:S(2)}) async-start(), calls=%async_computation.26 | async-start | bytes 540672
  692.6 579.9 %reduce-scatter.29.cloned.1.call-start = ((), (), s32[]{:S(2)}) async-start(), calls=%async_computation.22 | async-start | bytes 10485760 | tf_op jit(solution)/shard_map/reduce_scatter | solution.py:321
  700.0 720.1 %reduce-scatter.27.cloned.1.call-start = ((), (), s32[]{:S(2)}) async-start(), calls=%async_computation.21 | async-start | bytes 10485760 | tf_op jit(solution)/shard_map/reduce_scatter | solution.py:315
  707.0 857.6 %reduce-scatter.25.cloned.1.call-start = ((), (), s32[]{:S(2)}) async-start(), calls=%async_computation.20 | async-start | bytes 4325376 | tf_op jit(solution)/shard_map/reduce_scatter | solution.py:309
  710.7 1011.7 %reduce-scatter.23.cloned.1.call-start = ((), (), s32[]{:S(2)}) async-start(), calls=%async_computation.19 | async-start | bytes 12976128 | tf_op jit(solution)/shard_map/reduce_scatter | solution.py:308
  (15 other events, 24.2 us)
Sparse Core Ops, SparseCore 0:
  10.9 72.2 all-gather.8
  96.1 102.7 all-gather.10
  201.7 60.7 all-gather.12
  263.9 193.2 all-gather.14
  458.7 147.8 all-gather.16
  640.8 40.2 reduce-scatter.30
  683.4 133.3 reduce-scatter.32
  819.1 15.5 reduce-scatter.40
  837.1 25.3 reduce-scatter.38
  865.1 132.4 reduce-scatter.34
  999.9 129.9 reduce-scatter.36
  1132.1 140.3 reduce-scatter.28
  1274.9 145.1 reduce-scatter.26
  1422.8 141.7 reduce-scatter.24
  1571.0 151.2 reduce-scatter.22
